TPU v7x, 32 devices: a whole 2x2x4 slice. The times are simulated.
32 devices in a mesh: outer: 4 (over y, x), inner: 8 (over z, core).
Axes of the slice: x: 2, y: 2, z: 4, core: 2. Of those that a mesh axis runs over, the one named last changes fastest.
Arguments:
- inputs: bfloat16 [8192, 8192], P(('outer', 'inner')), may hold values from -6 to 6
- step_size: float32 [8192, 128], P(('outer', 'inner')), may hold values from 0 to 1
- log_decay: float32 [8192, 128], P(('outer', 'inner')), may hold values from -1.25 to 0
- b_matrix: bfloat16 [8192, 1024], P(('outer', 'inner')), may hold values from -1 to 1
- c_matrix: bfloat16 [8192, 1024], P(('outer', 'inner')), may hold values from -1 to 1
- skip_gain: float32 [128], replicated, may hold values from 0.5 to 1.5
Outputs:
- mixed: bfloat16 [8192, 8192], P(('outer', 'inner'))
All inputs are finite; a program needn't handle non-finite values.
Results may differ from a plain program's by a relative error of at most 0.006.
Values may be sent and summed in bfloat16 or wider, within the bound.
No kernel may reach another device: no remote copies, remote signals or barrier semaphores. Data moves between devices by JAX's collectives and lax.ppermute only.
A program may use at most 128 MiB of HBM per device.

v0:
```python
import jax
import jax.numpy as jnp
from jax import lax
from jax.sharding import PartitionSpec as P

GROUPS = 8
BLOCK_LENGTH = 256
MIXED_PREC = lax.Precision.HIGH


def passed_along(block, axis, distance):
    devices = range(lax.axis_size(axis))
    route = [(i - distance, i) for i in devices if i - distance in devices]
    return lax.ppermute(block, axis, route)


def group_pass(scaled, decay_log, b_rows, c_rows):
    seq_rows, head_count, head_width = scaled.shape
    state_width = b_rows.shape[1]
    block_rows = min(BLOCK_LENGTH, seq_rows)
    per_turn = min(8, seq_rows // block_rows)
    turn_count = seq_rows // (block_rows * per_turn)
    lower_mask = jnp.tril(jnp.ones((block_rows, block_rows), dtype=bool))

    def advance(carried_pair, pieces):
        carried, offset = carried_pair
        scaled_part, log_part, b_part, c_part = pieces
        running = jnp.cumsum(log_part, axis=1)
        scores = jnp.einsum("ktn,ksn->kts", c_part, b_part, preferred_element_type=jnp.float32)
        spread = running[:, :, None, :] - running[:, None, :, :]
        weights = scores[..., None] * jnp.exp(
            jnp.where(lower_mask[None, :, :, None], spread, -jnp.inf)
        )
        as_float = scaled_part.astype(jnp.float32)
        within = jnp.einsum("ktsh,kshp->kthp", weights, as_float, precision=MIXED_PREC)
        span_total = running[:, -1, :]
        to_end = jnp.exp(span_total[:, None, :] - running)
        local_states = jnp.einsum(
            "kshp,ksn->khpn",
            as_float * to_end[..., None],
            b_part.astype(jnp.float32),
            precision=MIXED_PREC,
        )
        entering = []
        for member in range(per_turn):
            entering.append(carried)
            carried = jnp.exp(span_total[member])[:, None, None] * carried + local_states[member]
        entering = jnp.stack(entering)
        from_carry = (
            jnp.einsum("ktn,khpn->kthp", c_part.astype(jnp.float32), entering, precision=MIXED_PREC)
            * jnp.exp(running)[..., None]
        )
        before = jnp.cumsum(span_total, axis=0) - span_total + offset[None, :]
        return (
            (carried, offset + jnp.sum(span_total, axis=0)),
            (within + from_carry, running + before[:, None, :]),
        )

    start_pair = (
        jnp.zeros((head_count, head_width, state_width), jnp.float32),
        jnp.zeros((head_count,), jnp.float32),
    )
    pieces = (
        scaled.reshape(turn_count, per_turn, block_rows, head_count, head_width),
        decay_log.reshape(turn_count, per_turn, block_rows, head_count),
        b_rows.reshape(turn_count, per_turn, block_rows, state_width),
        c_rows.reshape(turn_count, per_turn, block_rows, state_width),
    )
    (end_state, block_log), (outputs, running_all) = lax.scan(advance, start_pair, pieces)
    return (
        outputs.reshape(seq_rows, head_count, head_width),
        end_state,
        block_log,
        running_all.reshape(seq_rows, head_count),
    )


def carry_chain(block_log, end_state):
    incoming = jnp.zeros_like(end_state)
    for handoff_turn in range(lax.axis_size("outer") - 1):
        incoming = passed_along(
            jnp.exp(block_log)[:, None, None] * incoming + end_state, "outer", 1
        )
    return incoming


def local(inputs, step_size, log_decay, b_matrix, c_matrix, skip_gain):
    tokens = inputs.shape[0]
    head_count = step_size.shape[1]
    head_width = inputs.shape[1] // head_count
    state_width = b_matrix.shape[1] // GROUPS
    inner_count = lax.axis_size("inner")
    heads_dev = head_count // inner_count
    copies = inner_count // GROUPS
    b_copy = jnp.repeat(b_matrix.reshape(tokens, GROUPS, state_width), copies, axis=1).reshape(
        tokens, inner_count * state_width
    )
    c_copy = jnp.repeat(c_matrix.reshape(tokens, GROUPS, state_width), copies, axis=1).reshape(
        tokens, inner_count * state_width
    )
    head_inputs, b_rows, c_rows = (
        lax.all_to_all(inputs, "inner", split_axis=1, concat_axis=0, tiled=True),
        lax.all_to_all(b_copy, "inner", split_axis=1, concat_axis=0, tiled=True),
        lax.all_to_all(c_copy, "inner", split_axis=1, concat_axis=0, tiled=True),
    )
    step_rates, decay_log = (
        lax.all_to_all(step_size, "inner", split_axis=1, concat_axis=0, tiled=True),
        lax.all_to_all(log_decay, "inner", split_axis=1, concat_axis=0, tiled=True),
    )
    seq_rows = head_inputs.shape[0]
    head_inputs = head_inputs.reshape(seq_rows, heads_dev, head_width)
    scaled = (head_inputs.astype(jnp.float32) * step_rates[:, :, None]).astype(jnp.bfloat16)
    outputs, end_state, block_log, running_all = group_pass(scaled, decay_log, b_rows, c_rows)
    incoming = carry_chain(block_log, end_state)
    carried_term = (
        jnp.einsum("tn,hpn->thp", c_rows.astype(jnp.float32), incoming, precision=MIXED_PREC)
        * jnp.exp(running_all)[:, :, None]
    )
    skip_local = lax.dynamic_slice_in_dim(skip_gain, lax.axis_index("inner") * heads_dev, heads_dev)
    mixed_out = outputs + carried_term + skip_local[None, :, None] * head_inputs.astype(jnp.float32)
    mixed_out = mixed_out.astype(jnp.bfloat16).reshape(seq_rows, heads_dev * head_width)
    return lax.all_to_all(mixed_out, "inner", split_axis=0, concat_axis=1, tiled=True)


def solution(mesh):
    placed = (
        P(("outer", "inner"), None),
        P(("outer", "inner"), None),
        P(("outer", "inner"), None),
        P(("outer", "inner"), None),
        P(("outer", "inner"), None),
        P(),
    )
    return jax.shard_map(
        local, mesh=mesh, in_specs=placed, out_specs=P(("outer", "inner"), None), check_vma=False
    )
```

profile of v0, /device:TPU:0, one launch (start us, length us, event | category | flops | bytes accessed | tf_op | source)
XLA Modules:
  0.0 358.2 jit_solution(7346321738298869880)
XLA Ops:
  0.0 1.6 copy.51
  1.6 6.4 %all-to-all-start.4 = ((f32[256,8,16]{0,2,1:T(8,128)}), f32[256,8,16]{0,2,1:T(8,128)S(1)}, u32[]{:S(2)}, u32[]{:S(2)}) async-start(f32[256,8,16]{0,2,1:T(8,128)} %bitcast.9), calls=%async_computation.4 | async-start | bytes 262144 | tf_op jit(solution)/shard_map/all_to_all | solution.py:108
  8.0 1.2 copy.49
  9.2 1.0 copy.50
  10.2 4.5 %all-to-all-done.4 = f32[256,8,16]{0,2,1:T(8,128)S(1)} async-done(((f32[256,8,16]{0,2,1:T(8,128)}), f32[256,8,16]{0,2,1:T(8,128)S(1)}, u32[]{:S(2)}, u32[]{:S(2)}) %all-to-all-start.4) | async-done | bytes 131104 | tf_op jit(solution)/shard_map/all_to_all | solution.py:108
  14.7 3.5 all-to-all-start.3
  18.2 1.2 copy.47
  19.5 1.0 copy.48
  20.5 13.0 %all-to-all-done.3 = bf16[256,8,128]{2,0,1:T(8,128)(2,1)S(1)} async-done(((bf16[256,8,128]{2,0,1:T(8,128)(2,1)}), bf16[256,8,128]{2,0,1:T(8,128)(2,1)S(1)}, u32[]{:S(2)}, u32[]{:S(2)}) %all-to-all-start.3) | async-done | bytes 524320 | tf_op jit(solution)/shard_map/all_to_all | solution.py:103
  33.5 3.5 all-to-all-start.2
  37.0 6.4 %copy.45 = bf16[256,8192]{0,1:T(8,128)(2,1)} copy(bf16[256,8192]{1,0:T(8,128)(2,1)} %param.6) | data formatting | bytes 8388608 | tf_op args[0]
  43.4 8.9 %all-to-all-done.2 = bf16[256,8,128]{2,0,1:T(8,128)(2,1)S(1)} async-done(((bf16[256,8,128]{2,0,1:T(8,128)(2,1)}), bf16[256,8,128]{2,0,1:T(8,128)(2,1)S(1)}, u32[]{:S(2)}, u32[]{:S(2)}) %all-to-all-start.2) | async-done | bytes 524320 | tf_op jit(solution)/shard_map/all_to_all | solution.py:104
  52.3 4.7 %all-to-all-start = ((bf16[256,8,1024]{0,2,1:T(8,128)(2,1)}), bf16[256,8,1024]{0,2,1:T(8,128)(2,1)}, u32[]{:S(2)}, u32[]{:S(2)}) async-start(bf16[256,8,1024]{0,2,1:T(8,128)(2,1)} %bitcast.156), calls=%async_computation | async-start | bytes 8388608 | tf_op jit(solution)/shard_map/all_to_all | solution.py:102
  59.8 4.6 %reduce-window.6 = f32[8,16,2,128]{3,1,2,0:T(8,128)S(1)} reduce-window(f32[8,16,2,128]{3,1,2,0:T(8,128)S(1)} %copy_bitcast_fusion, f32[]{:T(128)} %constant.19.clone.1), window={size=1x1x1x128 pad=0_0x0_0x0_0x127_0}, to_apply=%region_0.1 | reduce-window | flops 4161536 | bytes 262148 | tf_op jit(solution)/shard_map/reduce-window
  67.9 83.0 %all-to-all-done = bf16[256,8,1024]{0,2,1:T(8,128)(2,1)} async-done(((bf16[256,8,1024]{0,2,1:T(8,128)(2,1)}), bf16[256,8,1024]{0,2,1:T(8,128)(2,1)}, u32[]{:S(2)}, u32[]{:S(2)}) %all-to-all-start) | async-done | bytes 4194336 | tf_op jit(solution)/shard_map/all_to_all | solution.py:102
  150.9 3.4 all-to-all-start.1
  154.3 9.6 %convert_bitcast_fusion = (f32[8,256,1024]{1,2,0:T(8,128)}, f32[256,8,1024]{0,2,1:T(8,128)}) fusion(bf16[256,8,1024]{0,2,1:T(8,128)(2,1)} %all-to-all-done), kind=kLoop, calls=%fused_computation.22 | loop fusion | flops 2097152 | bytes 20971520 | tf_op jit(solution)/shard_map/convert_element_type | solution.py:112
  164.0 6.1 %fusion.15 = f32[8,16,64,128]{3,2,1,0:T(8,128)S(1)} fusion(f32[8,256,16]{1,2,0:T(8,128)} %get-tuple-element.56, f32[8,256,16,64]{1,3,2,0:T(8,128)} %bitcast.153, f32[8,256,16]{1,2,0:T(8,128)S(1)} %bitcast.163, bf16[256,8,128]{2,0,1:T(8,128)(2,1)S(1)} %all-to-all-done.3), kind=kOutput, calls=%fused_computation.17 | convolution fusion | flops 1619001344 | bytes 13369344 | tf_op jit(solution)/shard_map/while/body/eval_jaxpr/kshp,ksn->khpn/dot_general | solution.py:38
  170.5 3.7 %collective-permute-start = (f32[16,64,128]{2,1,0:T(8,128)S(1)}, f32[16,64,128]{2,1,0:T(8,128)S(1)}, u32[]{:S(2)}, u32[]{:S(2)}) collective-permute-start(f32[16,64,128]{2,1,0:T(8,128)S(1)} %get-tuple-element.45), channel_id=1, source_target_pairs={{0,8},{8,16},{16,24},{1,9},{9,17},{17,25},{2,10},{10,18},{18,26},{... | collective-permute-start | bytes 1572872 | tf_op jit(solution)/shard_map/ppermute | solution.py:14
  174.7 17.2 %fusion = f32[8,16,64,256]{3,2,1,0:T(8,128)} fusion(f32[8,256,16]{1,2,0:T(8,128)S(1)} %bitcast_bitcast_fusion, f32[8,256,256]{2,1,0:T(8,128)S(1)} %fusion.29, pred[256,256]{1,0:T(8,128)(4,1)S(1)} %copy-done.5, f32[8,256,16,64]{1,3,2,0:T(8,128)S(1)} %bitcast.154, f32[8,256,16]{1,2,0:T(8,128)S(1)} %bitcast.164), kind=kOutput, calls=%fused_computation | convolution fusion | flops 3250585600 | bytes 19202048 | tf_op jit(solution)/shard_map/while/body/eval_jaxpr/ktsh,kshp->kthp/dot_general | solution.py:35
  192.6 3.4 collective-permute-start.1
  196.3 2.0 copy-done.2
  198.3 9.1 %collective-permute-done.1 = f32[16,64,128]{2,1,0:T(8,128)S(1)} collective-permute-done((f32[16,64,128]{2,1,0:T(8,128)S(1)}, f32[16,64,128]{2,1,0:T(8,128)S(1)}, u32[]{:S(2)}, u32[]{:S(2)}) %collective-permute-start.1) | collective-permute-done | bytes 524320 | tf_op jit(solution)/shard_map/ppermute | solution.py:14
  207.6 4.9 %collective-permute-start.2 = (f32[16,64,128]{2,1,0:T(8,128)S(1)}, f32[16,64,128]{2,1,0:T(8,128)S(1)}, u32[]{:S(2)}, u32[]{:S(2)}) collective-permute-start(f32[16,64,128]{2,1,0:T(8,128)S(1)} %multiply_add_fusion), channel_id=1, source_target_pairs={{0,8},{8,16},{16,24},{1,9},{9,17},{17,25},{2,10},{10,18},{18,26},{... | collective-permute-start | bytes 1572872 | tf_op jit(solution)/shard_map/ppermute | solution.py:14
  212.4 7.8 %fusion.14 = f32[8,16,8,8,256]{4,3,2,1,0:T(8,128)S(1)} fusion(f32[8,16,64,256]{3,2,1,0:T(8,128)} %fusion, f32[8,256,16]{1,2,0:T(8,128)S(1)} %copy-done.3, f32[8,16,64,128]{3,2,1,0:T(8,128)} %copy-done.2, bf16[256,8,128]{2,0,1:T(8,128)(2,1)S(1)} %all-to-all-done.2), kind=kOutput, calls=%fused_computation.16 | convolution fusion | flops 1614807040 | bytes 21626880 | tf_op jit(solution)/shard_map/while/body/eval_jaxpr/ktn,khpn->kthp/dot_general | solution.py:50
  220.3 4.3 %copy.65 = f32[8,16,8,8,256]{4,3,0,2,1:T(8,128)} copy(f32[8,16,8,8,256]{4,3,2,1,0:T(8,128)S(1)} %fusion.14) | data formatting | bytes 16777216 | tf_op jit(solution)/shard_map/reshape | solution.py:71
  224.5 8.1 %copy.58 = f32[8,256,1024]{1,0,2:T(8,128)} copy(f32[8,256,1024]{1,2,0:T(8,128)S(1)} %bitcast.152) | data formatting | bytes 16777216 | tf_op jit(solution)/shard_map/convert_element_type | solution.py:112
  232.6 9.3 %reshape.159 = f32[2048,16,64]{0,2,1:T(8,128)} reshape(f32[8,256,1024]{1,0,2:T(8,128)} %copy.58) | data formatting | bytes 16777216 | tf_op jit(solution)/shard_map/convert_element_type | solution.py:112
  241.9 9.0 %fusion.12 = bf16[2048,16,64]{0,2,1:T(8,128)(2,1)S(1)} fusion(f32[2048,16,64]{0,2,1:T(8,128)} %bitcast.150, f32[2048,16,64]{0,2,1:T(8,128)} %reshape.159, f32[16,64,128]{2,1,0:T(8,128)S(1)} %collective-permute-done.2, bf16[2048,128,1]{1,0,2:T(8,128)(2,1)S(1)} %bitcast.159, f32[16]{0:T(128)S(1)} %copy-done.11, f32[2048,16]{0,1:T(8,128)S(1)} %bitcast.162), kind=kOutput, calls=%fused_computation.13 | convolution fusion | flops 1621098496 | bytes 22151232 | tf_op jit(solution)/shard_map/tn,hpn->thp/dot_general | solution.py:116
  250.9 1.5 copy.67
  253.3 98.6 %all_to_all.90 = bf16[8,256,1024]{1,2,0:T(8,128)(2,1)} all-to-all(bf16[8,256,1024]{1,2,0:T(8,128)(2,1)S(1)} %copy.59), channel_id=1, replica_groups=mesh['outer'=4,'inner'=8] {'inner'}, dimensions={0} | all-to-all | bytes 8388608 | tf_op jit(solution)/shard_map/all_to_all | solution.py:122
  351.9 6.3 %copy.60 = bf16[256,8192]{1,0:T(8,128)(2,1)} copy(bf16[256,8192]{0,1:T(8,128)(2,1)} %bitcast.158) | data formatting | bytes 8388608 | tf_op jit(solution)/shard_map/all_to_all | solution.py:122
  (64 shorter events, 9.2 us)
Async XLA Ops:
  1.6 13.1 %all-to-all-start.4 = ((f32[256,8,16]{0,2,1:T(8,128)}), f32[256,8,16]{0,2,1:T(8,128)S(1)}, u32[]{:S(2)}, u32[]{:S(2)}) async-start(f32[256,8,16]{0,2,1:T(8,128)} %bitcast.9), calls=%async_computation.4 | async-start | bytes 262144 | tf_op jit(solution)/shard_map/all_to_all | solution.py:108
  14.7 18.8 %all-to-all-start.3 = ((bf16[256,8,128]{2,0,1:T(8,128)(2,1)}), bf16[256,8,128]{2,0,1:T(8,128)(2,1)S(1)}, u32[]{:S(2)}, u32[]{:S(2)}) async-start(bf16[256,8,128]{2,0,1:T(8,128)(2,1)} %copy.50), calls=%async_computation.3 | async-start | bytes 1048576 | tf_op jit(solution)/shard_map/all_to_all | solution.py:103
  33.5 18.8 %all-to-all-start.2 = ((bf16[256,8,128]{2,0,1:T(8,128)(2,1)}), bf16[256,8,128]{2,0,1:T(8,128)(2,1)S(1)}, u32[]{:S(2)}, u32[]{:S(2)}) async-start(bf16[256,8,128]{2,0,1:T(8,128)(2,1)} %copy.48), calls=%async_computation.2 | async-start | bytes 1048576 | tf_op jit(solution)/shard_map/all_to_all | solution.py:104
  52.3 4.7 %copy-start.4 = (f32[256,128]{1,0:T(8,128)S(1)}, f32[256,128]{1,0:T(8,128)}, u32[]{:S(2)}) copy-start(f32[256,128]{1,0:T(8,128)} %param.7) | copy-start | bytes 393220
  52.3 5.5 %copy-start.13 = (f32[128]{0:T(128)S(1)}, f32[128]{0:T(128)}, u32[]{:S(2)}) copy-start(f32[128]{0:T(128)} %param.11) | copy-start | bytes 1540
  52.3 98.7 %all-to-all-start = ((bf16[256,8,1024]{0,2,1:T(8,128)(2,1)}), bf16[256,8,1024]{0,2,1:T(8,128)(2,1)}, u32[]{:S(2)}, u32[]{:S(2)}) async-start(bf16[256,8,1024]{0,2,1:T(8,128)(2,1)} %bitcast.156), calls=%async_computation | async-start | bytes 8388608 | tf_op jit(solution)/shard_map/all_to_all | solution.py:102
  150.9 13.0 %all-to-all-start.1 = ((f32[256,8,16]{0,2,1:T(8,128)}), f32[256,8,16]{0,2,1:T(8,128)S(1)}, u32[]{:S(2)}, u32[]{:S(2)}) async-start(f32[256,8,16]{0,2,1:T(8,128)} %bitcast.165), calls=%async_computation.1 | async-start | bytes 262144 | tf_op jit(solution)/shard_map/all_to_all | solution.py:107
  163.9 6.2 %copy-start.6 = (f32[16]{0:T(128)S(1)}, f32[16]{0:T(128)}, u32[]{:S(2)}) copy-start(f32[16]{0:T(128)} %get-tuple-element.27) | copy-start | bytes 196
  163.9 6.2 %copy-start.7 = (f32[16]{0:T(128)S(1)}, f32[16]{0:T(128)}, u32[]{:S(2)}) copy-start(f32[16]{0:T(128)} %get-tuple-element.29) | copy-start | bytes 196
  163.9 6.2 %copy-start.8 = (f32[16]{0:T(128)S(1)}, f32[16]{0:T(128)}, u32[]{:S(2)}) copy-start(f32[16]{0:T(128)} %get-tuple-element.42) | copy-start | bytes 196
  163.9 6.2 %copy-start.10 = (f32[16]{0:T(128)S(1)}, f32[16]{0:T(128)}, u32[]{:S(2)}) copy-start(f32[16]{0:T(128)} %get-tuple-element.25) | copy-start | bytes 196
  163.9 6.2 %copy-start.12 = (f32[16]{0:T(128)S(1)}, f32[16]{0:T(128)}, u32[]{:S(2)}) copy-start(f32[16]{0:T(128)} %get-tuple-element.59) | copy-start | bytes 196
  163.9 10.3 %copy-start.1 = (f32[8,16,64,128]{3,2,1,0:T(8,128)S(1)}, f32[8,16,64,128]{3,2,1,0:T(8,128)}, u32[]{:S(2)}) copy-start(f32[8,16,64,128]{3,2,1,0:T(8,128)} %broadcast_dynamic-update-slice_fusion) | copy-start | bytes 12582916
  170.1 4.6 %copy-start = (f32[256,8,1024]{0,2,1:T(8,128)S(1)}, f32[256,8,1024]{0,2,1:T(8,128)}, u32[]{:S(2)}) copy-start(f32[256,8,1024]{0,2,1:T(8,128)} %get-tuple-element.54) | copy-start | bytes 25165828
  170.1 4.6 %copy-start.5 = (pred[256,256]{1,0:T(8,128)(4,1)S(1)}, pred[256,256]{1,0:T(8,128)(4,1)}, u32[]{:S(2)}) copy-start(pred[256,256]{1,0:T(8,128)(4,1)} %iota_compare_fusion) | copy-start | bytes 196612
  170.5 21.7 %collective-permute-start = (f32[16,64,128]{2,1,0:T(8,128)S(1)}, f32[16,64,128]{2,1,0:T(8,128)S(1)}, u32[]{:S(2)}, u32[]{:S(2)}) collective-permute-start(f32[16,64,128]{2,1,0:T(8,128)S(1)} %get-tuple-element.45), channel_id=1, source_target_pairs={{0,8},{8,16},{16,24},{1,9},{9,17},{17,25},{2,10},{10,18},{18,26},{... | collective-permute-start | bytes 1572872 | tf_op jit(solution)/shard_map/ppermute | solution.py:14
  191.8 0.6 copy-start.9
  192.1 20.4 %copy-start.3 = (f32[8,256,16]{1,2,0:T(8,128)S(1)}, f32[8,256,16]{1,2,0:T(8,128)}, u32[]{:S(2)}) copy-start(f32[8,256,16]{1,2,0:T(8,128)} %get-tuple-element.57) | copy-start | bytes 393220
  192.6 14.8 %collective-permute-start.1 = (f32[16,64,128]{2,1,0:T(8,128)S(1)}, f32[16,64,128]{2,1,0:T(8,128)S(1)}, u32[]{:S(2)}, u32[]{:S(2)}) collective-permute-start(f32[16,64,128]{2,1,0:T(8,128)S(1)} %multiply_add_fusion.1), channel_id=1, source_target_pairs={{0,8},{8,16},{16,24},{1,9},{9,17},{17,25},{2,10},{10,18},{18,26},{... | collective-permute-start | bytes 1572872 | tf_op jit(solution)/shard_map/ppermute | solution.py:14
  196.3 2.0 copy-start.2
  207.4 17.1 %slice-start = ((s8[8388608]{0:T(1024)(128)(4,1)}), s8[4194304]{0:T(1024)(128)(4,1)S(1)}, s32[]{:S(2)}) async-start(s8[8388608]{0:T(1024)(128)(4,1)} %bitcast.151), calls=%async_computation.6 | async-start | bytes 8388608
  207.6 34.3 %collective-permute-start.2 = (f32[16,64,128]{2,1,0:T(8,128)S(1)}, f32[16,64,128]{2,1,0:T(8,128)S(1)}, u32[]{:S(2)}, u32[]{:S(2)}) collective-permute-start(f32[16,64,128]{2,1,0:T(8,128)S(1)} %multiply_add_fusion), channel_id=1, source_target_pairs={{0,8},{8,16},{16,24},{1,9},{9,17},{17,25},{2,10},{10,18},{18,26},{... | collective-permute-start | bytes 1572872 | tf_op jit(solution)/shard_map/ppermute | solution.py:14
  212.4 12.1 %slice-start.1 = ((s8[8388608]{0:T(1024)(128)(4,1)}), s8[4194304]{0:T(1024)(128)(4,1)S(1)}, s32[]{:S(2)}) async-start(s8[8388608]{0:T(1024)(128)(4,1)} %bitcast.151), calls=%async_computation.7 | async-start | bytes 8388608
  232.6 9.3 %copy-start.11 = (f32[16]{0:T(128)S(1)}, f32[16]{0:T(128)}, u32[]{:S(2)}) copy-start(f32[16]{0:T(128)} %dynamic_slice.14) | copy-start | bytes 196
where the time goes:
time: 359 us; the launch traced here: 358 us
  waiting for transfers between devices  119 us (33%)
  blocking collectives  98.6 us (27%)
  local copies, waits for them, and re-layouts  47.6 us (13%)
  matrix products  40.5 us (11%)
  starting transfers between devices  33.4 us (9%)
  other arithmetic  19.2 us (5%)
    all_to_all x1, blocking collectives, local(): lax.all_to_all(mixed_out, 'inner', split_axis=0, concat_axis=1, tiled=True)  98.6 us
    all_to_all x1, waiting for transfers between devices, local(): lax.all_to_all(inputs, 'inner', split_axis=1, concat_axis=0, tiled=True)  83 us
    convert_element_type x2, local copies, waits for them, and re-layouts, local(): head_inputs.astype(jnp.float32) * step_rates[:, :, None]  17.4 us
    dot_general x1, matrix products, advance(): jnp.einsum('ktsh,kshp->kthp', weights, as_float, precision=MIXED_PREC)  17.2 us
    unnamed x39, local copies, waits for them, and re-layouts  15.9 us
    all_to_all x1, waiting for transfers between devices, local(): lax.all_to_all(b_copy, 'inner', split_axis=1, concat_axis=0, tiled=True)  13 us
    ppermute x3, starting transfers between devices, passed_along(): return lax.ppermute(block, axis, route)  12 us
    convert_element_type x1, other arithmetic, local(): head_inputs.astype(jnp.float32) * step_rates[:, :, None]  9.6 us
  transfers between devices with their start and end apart: 8, of which 5 were waited for; matrix products, arithmetic and copies ran while one was open for 22% of the time, Pallas kernels for 0%

commit v1 on v0

--- a/solution.py
+++ b/solution.py
@@ -6,6 +6,12 @@
 GROUPS = 8
 BLOCK_LENGTH = 256
 MIXED_PREC = lax.Precision.HIGH
+
+
+def swap_blocks(block, name, split, join):
+    cells = jnp.split(block, lax.axis_size(name), axis=split)
+    arrived = lax.all_to_all(jnp.stack(cells), name, 0, 0)
+    return jnp.concatenate(arrived, axis=join)
 
 
 def passed_along(block, axis, distance):
@@ -119,7 +125,7 @@
     skip_local = lax.dynamic_slice_in_dim(skip_gain, lax.axis_index("inner") * heads_dev, heads_dev)
     mixed_out = outputs + carried_term + skip_local[None, :, None] * head_inputs.astype(jnp.float32)
     mixed_out = mixed_out.astype(jnp.bfloat16).reshape(seq_rows, heads_dev * head_width)
-    return lax.all_to_all(mixed_out, "inner", split_axis=0, concat_axis=1, tiled=True)
+    return swap_blocks(mixed_out, "inner", 0, 1)
 
 
 def solution(mesh):

time: 359 us -> 358 us (level)
    all_to_all x2 -> x0, local copies, waits for them, and re-layouts: 7.18 us -> none  [local(): lax.all_to_all(mixed_out, 'inner', split_axis=0, concat_axis=1, tiled=True)]
    reshape x1 -> x2, local copies, waits for them, and re-layouts: 0.01 us -> 6.32 us  [the longest x1 6.32 us: swap_blocks(): return jnp.concatenate(arrived, axis=join)]
    unnamed x39 -> x45, local copies, waits for them, and re-layouts: 15.9 us -> 14.7 us
where the time goes in v1:
time: 358 us; the launch traced here: 357 us
  waiting for transfers between devices  119 us (33%)
  blocking collectives  98.6 us (28%)
  local copies, waits for them, and re-layouts  46.1 us (13%)
  matrix products  40.5 us (11%)
  starting transfers between devices  33.4 us (9%)
  other arithmetic  19.2 us (5%)
    all_to_all x1, blocking collectives, swap_blocks(): arrived = lax.all_to_all(jnp.stack(cells), name, 0, 0)  98.6 us
    all_to_all x1, waiting for transfers between devices, local(): lax.all_to_all(inputs, 'inner', split_axis=1, concat_axis=0, tiled=True)  83 us
    convert_element_type x2, local copies, waits for them, and re-layouts, local(): head_inputs.astype(jnp.float32) * step_rates[:, :, None]  17.4 us
    dot_general x1, matrix products, advance(): jnp.einsum('ktsh,kshp->kthp', weights, as_float, precision=MIXED_PREC)  17.2 us
    unnamed x45, local copies, waits for them, and re-layouts  14.7 us
    all_to_all x1, waiting for transfers between devices, local(): lax.all_to_all(b_copy, 'inner', split_axis=1, concat_axis=0, tiled=True)  13 us
    ppermute x3, starting transfers between devices, passed_along(): return lax.ppermute(block, axis, route)  12 us
    convert_element_type x1, other arithmetic, local(): head_inputs.astype(jnp.float32) * step_rates[:, :, None]  9.6 us
  transfers between devices with their start and end apart: 8, of which 5 were waited for; matrix products, arithmetic and copies ran while one was open for 22% of the time, Pallas kernels for 0%

profile of v1, /device:TPU:0, one launch (start us, length us, event | category | flops | bytes accessed | tf_op | source)
XLA Modules:
  0.0 356.8 jit_solution(176809697345480502)
XLA Ops:
  0.0 1.6 copy.51
  1.6 6.4 %all-to-all-start.4 = ((f32[256,8,16]{0,2,1:T(8,128)}), f32[256,8,16]{0,2,1:T(8,128)S(1)}, u32[]{:S(2)}, u32[]{:S(2)}) async-start(f32[256,8,16]{0,2,1:T(8,128)} %bitcast.9), calls=%async_computation.4 | async-start | bytes 262144 | tf_op jit(solution)/shard_map/all_to_all | solution.py:114
  8.0 1.2 copy.49
  9.2 1.0 copy.50
  10.2 4.5 %all-to-all-done.4 = f32[256,8,16]{0,2,1:T(8,128)S(1)} async-done(((f32[256,8,16]{0,2,1:T(8,128)}), f32[256,8,16]{0,2,1:T(8,128)S(1)}, u32[]{:S(2)}, u32[]{:S(2)}) %all-to-all-start.4) | async-done | bytes 131104 | tf_op jit(solution)/shard_map/all_to_all | solution.py:114
  14.7 3.5 all-to-all-start.3
  18.2 1.2 copy.47
  19.5 1.0 copy.48
  20.5 13.0 %all-to-all-done.3 = bf16[256,8,128]{2,0,1:T(8,128)(2,1)S(1)} async-done(((bf16[256,8,128]{2,0,1:T(8,128)(2,1)}), bf16[256,8,128]{2,0,1:T(8,128)(2,1)S(1)}, u32[]{:S(2)}, u32[]{:S(2)}) %all-to-all-start.3) | async-done | bytes 524320 | tf_op jit(solution)/shard_map/all_to_all | solution.py:109
  33.5 3.5 all-to-all-start.2
  37.0 6.4 %copy.45 = bf16[256,8192]{0,1:T(8,128)(2,1)} copy(bf16[256,8192]{1,0:T(8,128)(2,1)} %param.6) | data formatting | bytes 8388608 | tf_op args[0]
  43.4 8.9 %all-to-all-done.2 = bf16[256,8,128]{2,0,1:T(8,128)(2,1)S(1)} async-done(((bf16[256,8,128]{2,0,1:T(8,128)(2,1)}), bf16[256,8,128]{2,0,1:T(8,128)(2,1)S(1)}, u32[]{:S(2)}, u32[]{:S(2)}) %all-to-all-start.2) | async-done | bytes 524320 | tf_op jit(solution)/shard_map/all_to_all | solution.py:110
  52.3 4.7 %all-to-all-start = ((bf16[256,8,1024]{0,2,1:T(8,128)(2,1)}), bf16[256,8,1024]{0,2,1:T(8,128)(2,1)}, u32[]{:S(2)}, u32[]{:S(2)}) async-start(bf16[256,8,1024]{0,2,1:T(8,128)(2,1)} %bitcast.158), calls=%async_computation | async-start | bytes 8388608 | tf_op jit(solution)/shard_map/all_to_all | solution.py:108
  59.8 4.6 %reduce-window.6 = f32[8,16,2,128]{3,1,2,0:T(8,128)S(1)} reduce-window(f32[8,16,2,128]{3,1,2,0:T(8,128)S(1)} %copy_bitcast_fusion, f32[]{:T(128)} %constant.19.clone.1), window={size=1x1x1x128 pad=0_0x0_0x0_0x127_0}, to_apply=%region_0.1 | reduce-window | flops 4161536 | bytes 262148 | tf_op jit(solution)/shard_map/reduce-window
  65.2 0.8 exponential_bitcast_fusion
  67.9 83.0 %all-to-all-done = bf16[256,8,1024]{0,2,1:T(8,128)(2,1)} async-done(((bf16[256,8,1024]{0,2,1:T(8,128)(2,1)}), bf16[256,8,1024]{0,2,1:T(8,128)(2,1)}, u32[]{:S(2)}, u32[]{:S(2)}) %all-to-all-start) | async-done | bytes 4194336 | tf_op jit(solution)/shard_map/all_to_all | solution.py:108
  150.9 3.4 all-to-all-start.1
  154.3 9.6 %convert_bitcast_fusion = (f32[8,256,1024]{1,2,0:T(8,128)}, f32[256,8,1024]{0,2,1:T(8,128)}) fusion(bf16[256,8,1024]{0,2,1:T(8,128)(2,1)} %all-to-all-done), kind=kLoop, calls=%fused_computation.22 | loop fusion | flops 2097152 | bytes 20971520 | tf_op jit(solution)/shard_map/convert_element_type | solution.py:118
  164.0 6.1 %fusion.15 = f32[8,16,64,128]{3,2,1,0:T(8,128)S(1)} fusion(f32[8,256,16]{1,2,0:T(8,128)} %get-tuple-element.64, f32[8,256,16,64]{1,3,2,0:T(8,128)} %bitcast.156, f32[8,256,16]{1,2,0:T(8,128)S(1)} %bitcast.172, bf16[256,8,128]{2,0,1:T(8,128)(2,1)S(1)} %all-to-all-done.3), kind=kOutput, calls=%fused_computation.17 | convolution fusion | flops 1619001344 | bytes 13369344 | tf_op jit(solution)/shard_map/while/body/eval_jaxpr/kshp,ksn->khpn/dot_general | solution.py:44
  170.5 3.7 %collective-permute-start = (f32[16,64,128]{2,1,0:T(8,128)S(1)}, f32[16,64,128]{2,1,0:T(8,128)S(1)}, u32[]{:S(2)}, u32[]{:S(2)}) collective-permute-start(f32[16,64,128]{2,1,0:T(8,128)S(1)} %get-tuple-element.45), channel_id=1, source_target_pairs={{0,8},{8,16},{16,24},{1,9},{9,17},{17,25},{2,10},{10,18},{18,26},{... | collective-permute-start | bytes 1572872 | tf_op jit(solution)/shard_map/ppermute | solution.py:20
  174.7 17.2 %fusion = f32[8,16,64,256]{3,2,1,0:T(8,128)} fusion(f32[8,256,16]{1,2,0:T(8,128)S(1)} %bitcast_bitcast_fusion, f32[8,256,256]{2,1,0:T(8,128)S(1)} %fusion.29, pred[256,256]{1,0:T(8,128)(4,1)S(1)} %copy-done.5, f32[8,256,16,64]{1,3,2,0:T(8,128)S(1)} %bitcast.157, f32[8,256,16]{1,2,0:T(8,128)S(1)} %bitcast.173), kind=kOutput, calls=%fused_computation | convolution fusion | flops 3250585600 | bytes 19202048 | tf_op jit(solution)/shard_map/while/body/eval_jaxpr/ktsh,kshp->kthp/dot_general | solution.py:41
  192.6 3.4 collective-permute-start.1
  196.3 2.0 copy-done.2
  198.3 9.1 %collective-permute-done.1 = f32[16,64,128]{2,1,0:T(8,128)S(1)} collective-permute-done((f32[16,64,128]{2,1,0:T(8,128)S(1)}, f32[16,64,128]{2,1,0:T(8,128)S(1)}, u32[]{:S(2)}, u32[]{:S(2)}) %collective-permute-start.1) | collective-permute-done | bytes 524320 | tf_op jit(solution)/shard_map/ppermute | solution.py:20
  207.6 4.9 %collective-permute-start.2 = (f32[16,64,128]{2,1,0:T(8,128)S(1)}, f32[16,64,128]{2,1,0:T(8,128)S(1)}, u32[]{:S(2)}, u32[]{:S(2)}) collective-permute-start(f32[16,64,128]{2,1,0:T(8,128)S(1)} %multiply_add_fusion), channel_id=1, source_target_pairs={{0,8},{8,16},{16,24},{1,9},{9,17},{17,25},{2,10},{10,18},{18,26},{... | collective-permute-start | bytes 1572872 | tf_op jit(solution)/shard_map/ppermute | solution.py:20
  212.4 7.8 %fusion.14 = f32[8,16,8,8,256]{4,3,2,1,0:T(8,128)S(1)} fusion(f32[8,16,64,256]{3,2,1,0:T(8,128)} %fusion, f32[8,256,16]{1,2,0:T(8,128)S(1)} %copy-done.3, f32[8,16,64,128]{3,2,1,0:T(8,128)} %copy-done.2, bf16[256,8,128]{2,0,1:T(8,128)(2,1)S(1)} %all-to-all-done.2), kind=kOutput, calls=%fused_computation.16 | convolution fusion | flops 1614807040 | bytes 21626880 | tf_op jit(solution)/shard_map/while/body/eval_jaxpr/ktn,khpn->kthp/dot_general | solution.py:56
  220.3 4.3 %copy.65 = f32[8,16,8,8,256]{4,3,0,2,1:T(8,128)} copy(f32[8,16,8,8,256]{4,3,2,1,0:T(8,128)S(1)} %fusion.14) | data formatting | bytes 16777216 | tf_op jit(solution)/shard_map/reshape | solution.py:77
  224.5 8.1 %copy.58 = f32[8,256,1024]{1,0,2:T(8,128)} copy(f32[8,256,1024]{1,2,0:T(8,128)S(1)} %bitcast.155) | data formatting | bytes 16777216 | tf_op jit(solution)/shard_map/convert_element_type | solution.py:118
  232.6 9.3 %reshape.179 = f32[2048,16,64]{0,2,1:T(8,128)} reshape(f32[8,256,1024]{1,0,2:T(8,128)} %copy.58) | data formatting | bytes 16777216 | tf_op jit(solution)/shard_map/convert_element_type | solution.py:118
  241.9 9.0 %fusion.12 = bf16[2048,16,64]{0,2,1:T(8,128)(2,1)S(1)} fusion(f32[2048,16,64]{0,2,1:T(8,128)} %bitcast.153, f32[2048,16,64]{0,2,1:T(8,128)} %reshape.179, f32[16,64,128]{2,1,0:T(8,128)S(1)} %collective-permute-done.2, bf16[2048,128,1]{1,0,2:T(8,128)(2,1)S(1)} %bitcast.160, f32[16]{0:T(128)S(1)} %copy-done.11, f32[2048,16]{0,1:T(8,128)S(1)} %bitcast.171), kind=kOutput, calls=%fused_computation.13 | convolution fusion | flops 1621098496 | bytes 22151232 | tf_op jit(solution)/shard_map/tn,hpn->thp/dot_general | solution.py:122
  251.8 98.6 %all_to_all.76 = bf16[8,256,1024]{1,2,0:T(8,128)(2,1)} all-to-all(bf16[8,256,1024]{1,2,0:T(8,128)(2,1)S(1)} %constant_dynamic-update-slice_fusion.3), channel_id=1, replica_groups=mesh['outer'=4,'inner'=8] {'inner'}, dimensions={0} | all-to-all | bytes 8388608 | tf_op jit(solution)/shard_map/all_to_all | solution.py:13
  350.5 6.3 %copy.62 = bf16[256,8192]{1,0:T(8,128)(2,1)} copy(bf16[256,8192]{0,1:T(8,128)(2,1)} %bitcast.159) | data formatting | bytes 8388608 | tf_op jit(solution)/shard_map/reshape | solution.py:14
  (71 shorter events, 8.3 us)
Async XLA Ops:
  1.6 13.1 %all-to-all-start.4 = ((f32[256,8,16]{0,2,1:T(8,128)}), f32[256,8,16]{0,2,1:T(8,128)S(1)}, u32[]{:S(2)}, u32[]{:S(2)}) async-start(f32[256,8,16]{0,2,1:T(8,128)} %bitcast.9), calls=%async_computation.4 | async-start | bytes 262144 | tf_op jit(solution)/shard_map/all_to_all | solution.py:114
  14.7 18.8 %all-to-all-start.3 = ((bf16[256,8,128]{2,0,1:T(8,128)(2,1)}), bf16[256,8,128]{2,0,1:T(8,128)(2,1)S(1)}, u32[]{:S(2)}, u32[]{:S(2)}) async-start(bf16[256,8,128]{2,0,1:T(8,128)(2,1)} %copy.50), calls=%async_computation.3 | async-start | bytes 1048576 | tf_op jit(solution)/shard_map/all_to_all | solution.py:109
  33.5 18.8 %all-to-all-start.2 = ((bf16[256,8,128]{2,0,1:T(8,128)(2,1)}), bf16[256,8,128]{2,0,1:T(8,128)(2,1)S(1)}, u32[]{:S(2)}, u32[]{:S(2)}) async-start(bf16[256,8,128]{2,0,1:T(8,128)(2,1)} %copy.48), calls=%async_computation.2 | async-start | bytes 1048576 | tf_op jit(solution)/shard_map/all_to_all | solution.py:110
  52.3 4.7 %copy-start.4 = (f32[256,128]{1,0:T(8,128)S(1)}, f32[256,128]{1,0:T(8,128)}, u32[]{:S(2)}) copy-start(f32[256,128]{1,0:T(8,128)} %param.7) | copy-start | bytes 393220
  52.3 5.5 %copy-start.13 = (f32[128]{0:T(128)S(1)}, f32[128]{0:T(128)}, u32[]{:S(2)}) copy-start(f32[128]{0:T(128)} %param.11) | copy-start | bytes 1540
  52.3 98.7 %all-to-all-start = ((bf16[256,8,1024]{0,2,1:T(8,128)(2,1)}), bf16[256,8,1024]{0,2,1:T(8,128)(2,1)}, u32[]{:S(2)}, u32[]{:S(2)}) async-start(bf16[256,8,1024]{0,2,1:T(8,128)(2,1)} %bitcast.158), calls=%async_computation | async-start | bytes 8388608 | tf_op jit(solution)/shard_map/all_to_all | solution.py:108
  150.9 13.0 %all-to-all-start.1 = ((f32[256,8,16]{0,2,1:T(8,128)}), f32[256,8,16]{0,2,1:T(8,128)S(1)}, u32[]{:S(2)}, u32[]{:S(2)}) async-start(f32[256,8,16]{0,2,1:T(8,128)} %bitcast.174), calls=%async_computation.1 | async-start | bytes 262144 | tf_op jit(solution)/shard_map/all_to_all | solution.py:113
  163.9 6.2 %copy-start.6 = (f32[16]{0:T(128)S(1)}, f32[16]{0:T(128)}, u32[]{:S(2)}) copy-start(f32[16]{0:T(128)} %get-tuple-element.27) | copy-start | bytes 196
  163.9 6.2 %copy-start.7 = (f32[16]{0:T(128)S(1)}, f32[16]{0:T(128)}, u32[]{:S(2)}) copy-start(f32[16]{0:T(128)} %get-tuple-element.29) | copy-start | bytes 196
  163.9 6.2 %copy-start.8 = (f32[16]{0:T(128)S(1)}, f32[16]{0:T(128)}, u32[]{:S(2)}) copy-start(f32[16]{0:T(128)} %get-tuple-element.42) | copy-start | bytes 196
  163.9 6.2 %copy-start.10 = (f32[16]{0:T(128)S(1)}, f32[16]{0:T(128)}, u32[]{:S(2)}) copy-start(f32[16]{0:T(128)} %get-tuple-element.25) | copy-start | bytes 196
  163.9 6.2 %copy-start.12 = (f32[16]{0:T(128)S(1)}, f32[16]{0:T(128)}, u32[]{:S(2)}) copy-start(f32[16]{0:T(128)} %get-tuple-element.67) | copy-start | bytes 196
  163.9 10.3 %copy-start.1 = (f32[8,16,64,128]{3,2,1,0:T(8,128)S(1)}, f32[8,16,64,128]{3,2,1,0:T(8,128)}, u32[]{:S(2)}) copy-start(f32[8,16,64,128]{3,2,1,0:T(8,128)} %broadcast_dynamic-update-slice_fusion) | copy-start | bytes 12582916
  170.1 4.6 %copy-start = (f32[256,8,1024]{0,2,1:T(8,128)S(1)}, f32[256,8,1024]{0,2,1:T(8,128)}, u32[]{:S(2)}) copy-start(f32[256,8,1024]{0,2,1:T(8,128)} %get-tuple-element.62) | copy-start | bytes 25165828
  170.1 4.6 %copy-start.5 = (pred[256,256]{1,0:T(8,128)(4,1)S(1)}, pred[256,256]{1,0:T(8,128)(4,1)}, u32[]{:S(2)}) copy-start(pred[256,256]{1,0:T(8,128)(4,1)} %iota_compare_fusion) | copy-start | bytes 196612
  170.5 21.7 %collective-permute-start = (f32[16,64,128]{2,1,0:T(8,128)S(1)}, f32[16,64,128]{2,1,0:T(8,128)S(1)}, u32[]{:S(2)}, u32[]{:S(2)}) collective-permute-start(f32[16,64,128]{2,1,0:T(8,128)S(1)} %get-tuple-element.45), channel_id=1, source_target_pairs={{0,8},{8,16},{16,24},{1,9},{9,17},{17,25},{2,10},{10,18},{18,26},{... | collective-permute-start | bytes 1572872 | tf_op jit(solution)/shard_map/ppermute | solution.py:20
  191.8 0.6 copy-start.9
  192.1 20.4 %copy-start.3 = (f32[8,256,16]{1,2,0:T(8,128)S(1)}, f32[8,256,16]{1,2,0:T(8,128)}, u32[]{:S(2)}) copy-start(f32[8,256,16]{1,2,0:T(8,128)} %get-tuple-element.65) | copy-start | bytes 393220
  192.6 14.8 %collective-permute-start.1 = (f32[16,64,128]{2,1,0:T(8,128)S(1)}, f32[16,64,128]{2,1,0:T(8,128)S(1)}, u32[]{:S(2)}, u32[]{:S(2)}) collective-permute-start(f32[16,64,128]{2,1,0:T(8,128)S(1)} %multiply_add_fusion.1), channel_id=1, source_target_pairs={{0,8},{8,16},{16,24},{1,9},{9,17},{17,25},{2,10},{10,18},{18,26},{... | collective-permute-start | bytes 1572872 | tf_op jit(solution)/shard_map/ppermute | solution.py:20
  196.3 2.0 copy-start.2
  207.4 17.1 %slice-start = ((s8[8388608]{0:T(1024)(128)(4,1)}), s8[4194304]{0:T(1024)(128)(4,1)S(1)}, s32[]{:S(2)}) async-start(s8[8388608]{0:T(1024)(128)(4,1)} %bitcast.154), calls=%async_computation.6 | async-start | bytes 8388608
  207.6 34.3 %collective-permute-start.2 = (f32[16,64,128]{2,1,0:T(8,128)S(1)}, f32[16,64,128]{2,1,0:T(8,128)S(1)}, u32[]{:S(2)}, u32[]{:S(2)}) collective-permute-start(f32[16,64,128]{2,1,0:T(8,128)S(1)} %multiply_add_fusion), channel_id=1, source_target_pairs={{0,8},{8,16},{16,24},{1,9},{9,17},{17,25},{2,10},{10,18},{18,26},{... | collective-permute-start | bytes 1572872 | tf_op jit(solution)/shard_map/ppermute | solution.py:20
  212.4 12.1 %slice-start.1 = ((s8[8388608]{0:T(1024)(128)(4,1)}), s8[4194304]{0:T(1024)(128)(4,1)S(1)}, s32[]{:S(2)}) async-start(s8[8388608]{0:T(1024)(128)(4,1)} %bitcast.154), calls=%async_computation.7 | async-start | bytes 8388608
  232.6 9.3 %copy-start.11 = (f32[16]{0:T(128)S(1)}, f32[16]{0:T(128)}, u32[]{:S(2)}) copy-start(f32[16]{0:T(128)} %dynamic_slice.14) | copy-start | bytes 196
